TPU v7x, 512 devices: a whole 4x4x16 slice. The times are simulated.
512 devices in a mesh: dp: 64 (over y, z), mp: 8 (over x, core).
Axes of the slice: x: 4, y: 4, z: 16, core: 2. Of those that a mesh axis runs over, the one named last changes fastest.
Arguments:
- tokens_in: bfloat16 [8192, 8192], P('dp', 'mp'), may hold values from -6 to 6
- gate_pre: bfloat16 [8192, 28672], P('dp', 'mp'), may hold values from -8 to 8
- up_pre: bfloat16 [8192, 28672], P('dp', 'mp'), may hold values from -6 to 6
- hidden_grad: bfloat16 [8192, 28672], P('dp', 'mp'), may hold values from -160 to 160
- out_grad: bfloat16 [8192, 8192], P('dp', 'mp'), may hold values from -160 to 160
- proj_model: bfloat16 [8192, 128], P('mp'), may hold values from -0.0625 to 0.0625
- proj_hidden: bfloat16 [28672, 128], P('mp'), may hold values from -0.03125 to 0.03125
Outputs:
- whitened: float32 [64, 128, 64], P('dp', 'mp')
All inputs are finite; a program needn't handle non-finite values.
Results may differ from a plain program's by a relative error of at most 0.003.
Values sent between devices are 32-bit elements; how exact they have to be, the bound alone decides.
A program may use at most 64 MiB of HBM per device.

v0:
```python
import math
import jax
import jax.numpy as jnp
from jax import lax
from jax.sharding import PartitionSpec as P

RANK = 64
LEN = 128
highest = lax.Precision.HIGHEST


def partner_2(value, axis, apart):
    mask = 2**apart
    pairs = [(source, source ^ mask) for source in range(lax.axis_size(axis))]
    return lax.ppermute(value, axis, pairs)


def gradient_blocks(projected):
    columns_each = projected.shape[-1] // 4
    input_side = projected[..., :columns_each]
    output_side = projected[..., columns_each : 2 * columns_each]
    upward = projected[..., 2 * columns_each : 3 * columns_each]
    hidden_side = projected[..., 3 * columns_each :]
    up_block = jnp.einsum("elr,els->ers", input_side, upward, precision=highest)
    down_block = jnp.einsum("elr,els->ers", hidden_side, output_side, precision=highest)
    return jnp.concatenate([up_block, down_block], axis=1)


def gram_of(rows):
    flat_rows = rows.reshape(-1, rows.shape[-1])
    return jnp.dot(flat_rows.T, flat_rows, precision=highest, preferred_element_type=jnp.float32)


def shards(tokens_in, gate_pre, up_pre, hidden_grad, out_grad, proj_model, proj_hidden):
    gate_act = jax.nn.silu(gate_pre.astype(jnp.float32))
    up_grad = (hidden_grad.astype(jnp.float32) * gate_act).astype(jnp.bfloat16)
    hidden = (gate_act * up_pre.astype(jnp.float32)).astype(jnp.bfloat16)
    local_sums = jnp.concatenate(
        [
            jnp.dot(tokens_in, proj_model[:, :RANK], preferred_element_type=jnp.float32),
            jnp.dot(out_grad, proj_model[:, RANK:], preferred_element_type=jnp.float32),
            jnp.dot(up_grad, proj_hidden[:, :RANK], preferred_element_type=jnp.float32),
            jnp.dot(hidden, proj_hidden[:, RANK:], preferred_element_type=jnp.float32),
        ],
        axis=1,
    )
    local_examples = tokens_in.shape[0] // LEN
    shaped = local_sums.reshape(local_examples, LEN, 4 * RANK)
    model_shards = lax.axis_size("mp")
    rows_each = 2 * RANK // model_shards
    summed = lax.psum(shaped, "mp")
    blocks = gradient_blocks(summed)
    mine = lax.dynamic_slice_in_dim(blocks, lax.axis_index("mp") * rows_each, rows_each, 1)
    group_gram = gram_of(blocks)
    flat_mine = mine.reshape(local_examples * rows_each, RANK)
    lower = jnp.linalg.cholesky(group_gram)
    for level in range(lax.axis_size("dp").bit_length() - 1):
        partner = partner_2(lower, "dp", level)
        combined = jnp.dot(
            lower, lower.T, precision=highest, preferred_element_type=jnp.float32
        ) + jnp.dot(partner, partner.T, precision=highest, preferred_element_type=jnp.float32)
        lower = jnp.linalg.cholesky(combined)
    solved = jax.scipy.linalg.solve_triangular(lower, flat_mine.T, lower=True)
    factor = math.sqrt(local_examples * lax.axis_size("dp") * 2 * RANK)
    return (solved.T * factor).reshape(local_examples, rows_each, RANK)


def solution(mesh):
    in_specs = (
        P("dp", "mp"),
        P("dp", "mp"),
        P("dp", "mp"),
        P("dp", "mp"),
        P("dp", "mp"),
        P("mp", None),
        P("mp", None),
    )
    out_specs = P("dp", "mp", None)
    return jax.shard_map(shards, mesh=mesh, in_specs=in_specs, out_specs=out_specs, check_vma=False)
```

profile of v0, /device:TPU:8, one launch (start us, length us, event | category | flops | bytes accessed | tf_op | source)
XLA Modules:
  0.0 209.8 jit_solution(459969425136288152)
XLA Ops:
  6.6 2.7 %fusion.4 = f32[128,64]{0,1:T(8,128)S(1)} fusion(bf16[128,3584]{1,0:T(8,128)(2,1)} %param.11, bf16[3584,128]{1,0:T(8,128)(2,1)} %param.14, bf16[128,3584]{1,0:T(8,128)(2,1)} %param.9), kind=kOutput, calls=%fused_computation.17 | convolution fusion | flops 62390272 | bytes 2785280 | tf_op jit(solution)/shard_map/dot_general | solution.py:42
  9.3 1.0 fusion.5
  10.3 0.2 fusion.10
  10.6 0.4 fusion.8
  11.0 0.7 maximum_bitcast_fusion
  11.7 79.8 %all-reduce.2.cloned.1.call-done = f32[1,128,256]{1,2,0:T(8,128)} async-done(((f32[1,128,256]{1,2,0:T(8,128)}), f32[1,128,256]{1,2,0:T(8,128)}) %all-reduce.2.cloned.1.call-update) | async-done | bytes 131088 | tf_op jit(solution)/shard_map/psum | solution.py:51
  91.5 1.0 convolution_bitcast_fusion
  92.5 1.0 convolution_bitcast_fusion.1
  93.4 0.3 fusion.15
  93.8 5.8 %cholesky.119 = f32[64,64]{1,0:T(8,128)S(1)} custom-call(f32[64,64]{1,0:T(8,128)S(1)} %fusion.23), custom_call_target="Cholesky" | custom-call | tf_op jit(solution)/shard_map/jit(cholesky)/cholesky | solution.py:56
  99.7 0.6 compare_reduce_fusion.6
  100.3 0.7 select_select_fusion.6
  101.0 3.5 %collective-permute-start = (f32[64,64]{1,0:T(8,128)S(1)}, f32[64,64]{1,0:T(8,128)S(1)}, u32[]{:S(2)}, u32[]{:S(2)}) collective-permute-start(f32[64,64]{1,0:T(8,128)S(1)} %select_select_fusion.6), channel_id=1, source_target_pairs={{0,8},{8,0},{16,24},{24,16},{32,40},{40,32},{48,56},{56,48},{64,72... | collective-permute-start | bytes 49160 | tf_op jit(solution)/shard_map/ppermute | solution.py:15
  104.6 2.1 %collective-permute-done = f32[64,64]{1,0:T(8,128)S(1)} collective-permute-done((f32[64,64]{1,0:T(8,128)S(1)}, f32[64,64]{1,0:T(8,128)S(1)}, u32[]{:S(2)}, u32[]{:S(2)}) %collective-permute-start) | collective-permute-done | bytes 16416 | tf_op jit(solution)/shard_map/ppermute | solution.py:15
  106.8 0.2 convolution_add_fusion.5
  107.1 5.8 %cholesky.130 = f32[64,64]{1,0:T(8,128)S(1)} custom-call(f32[64,64]{1,0:T(8,128)S(1)} %fusion.22), custom_call_target="Cholesky" | custom-call | tf_op jit(solution)/shard_map/jit(cholesky)/cholesky | solution.py:62
  113.0 0.6 compare_reduce_fusion.5
  113.6 0.7 select_select_fusion.5
  114.3 4.5 %collective-permute-start.1 = (f32[64,64]{1,0:T(8,128)S(1)}, f32[64,64]{1,0:T(8,128)S(1)}, u32[]{:S(2)}, u32[]{:S(2)}) collective-permute-start(f32[64,64]{1,0:T(8,128)S(1)} %select_select_fusion.5), channel_id=1, source_target_pairs={{0,16},{8,24},{16,0},{24,8},{32,48},{40,56},{48,32},{56,40},{64,80... | collective-permute-start | bytes 49160 | tf_op jit(solution)/shard_map/ppermute | solution.py:15
  118.9 2.1 collective-permute-done.1
  121.0 0.2 convolution_add_fusion.4
  121.2 5.8 %cholesky.141 = f32[64,64]{1,0:T(8,128)S(1)} custom-call(f32[64,64]{1,0:T(8,128)S(1)} %fusion.21), custom_call_target="Cholesky" | custom-call | tf_op jit(solution)/shard_map/jit(cholesky)/cholesky | solution.py:62
  127.1 0.6 compare_reduce_fusion.4
  127.8 0.7 select_select_fusion.4
  128.4 7.6 %collective-permute-start.2 = (f32[64,64]{1,0:T(8,128)S(1)}, f32[64,64]{1,0:T(8,128)S(1)}, u32[]{:S(2)}, u32[]{:S(2)}) collective-permute-start(f32[64,64]{1,0:T(8,128)S(1)} %select_select_fusion.4), channel_id=1, source_target_pairs={{0,32},{8,40},{16,48},{24,56},{32,0},{40,8},{48,16},{56,24},{64,96... | collective-permute-start | bytes 49160 | tf_op jit(solution)/shard_map/ppermute | solution.py:15
  136.3 1.9 collective-permute-done.2
  138.2 0.2 convolution_add_fusion.3
  138.4 5.8 %cholesky.152 = f32[64,64]{1,0:T(8,128)S(1)} custom-call(f32[64,64]{1,0:T(8,128)S(1)} %fusion.20), custom_call_target="Cholesky" | custom-call | tf_op jit(solution)/shard_map/jit(cholesky)/cholesky | solution.py:62
  144.3 0.6 compare_reduce_fusion.3
  145.0 0.7 select_select_fusion.3
  145.6 14.1 %collective-permute-start.3 = (f32[64,64]{1,0:T(8,128)S(1)}, f32[64,64]{1,0:T(8,128)S(1)}, u32[]{:S(2)}, u32[]{:S(2)}) collective-permute-start(f32[64,64]{1,0:T(8,128)S(1)} %select_select_fusion.3), channel_id=1, source_target_pairs={{0,64},{8,72},{16,80},{24,88},{32,96},{40,104},{48,112},{56,120},{... | collective-permute-start | bytes 49160 | tf_op jit(solution)/shard_map/ppermute | solution.py:15
  159.9 1.7 collective-permute-done.3
  161.6 0.2 convolution_add_fusion.2
  161.9 5.8 %cholesky.163 = f32[64,64]{1,0:T(8,128)S(1)} custom-call(f32[64,64]{1,0:T(8,128)S(1)} %fusion.19), custom_call_target="Cholesky" | custom-call | tf_op jit(solution)/shard_map/jit(cholesky)/cholesky | solution.py:62
  167.8 0.6 compare_reduce_fusion.2
  168.4 0.7 select_select_fusion.2
  169.1 2.4 %collective-permute-start.4 = (f32[64,64]{1,0:T(8,128)S(1)}, f32[64,64]{1,0:T(8,128)S(1)}, u32[]{:S(2)}, u32[]{:S(2)}) collective-permute-start(f32[64,64]{1,0:T(8,128)S(1)} %select_select_fusion.2), channel_id=1, source_target_pairs={{0,128},{8,136},{16,144},{24,152},{32,160},{40,168},{48,176},{56,1... | collective-permute-start | bytes 49160 | tf_op jit(solution)/shard_map/ppermute | solution.py:15
  171.7 3.2 %collective-permute-done.4 = f32[64,64]{1,0:T(8,128)S(1)} collective-permute-done((f32[64,64]{1,0:T(8,128)S(1)}, f32[64,64]{1,0:T(8,128)S(1)}, u32[]{:S(2)}, u32[]{:S(2)}) %collective-permute-start.4) | collective-permute-done | bytes 16416 | tf_op jit(solution)/shard_map/ppermute | solution.py:15
  175.2 5.8 %cholesky.174 = f32[64,64]{1,0:T(8,128)S(1)} custom-call(f32[64,64]{1,0:T(8,128)S(1)} %fusion.18), custom_call_target="Cholesky" | custom-call | tf_op jit(solution)/shard_map/jit(cholesky)/cholesky | solution.py:62
  181.1 0.6 compare_reduce_fusion.1
  181.7 0.7 select_select_fusion.1
  182.4 4.0 %collective-permute-start.5 = (f32[64,64]{1,0:T(8,128)S(1)}, f32[64,64]{1,0:T(8,128)S(1)}, u32[]{:S(2)}, u32[]{:S(2)}) collective-permute-start(f32[64,64]{1,0:T(8,128)S(1)} %select_select_fusion.1), channel_id=1, source_target_pairs={{0,256},{8,264},{16,272},{24,280},{32,288},{40,296},{48,304},{56,3... | collective-permute-start | bytes 49160 | tf_op jit(solution)/shard_map/ppermute | solution.py:15
  186.6 3.1 %collective-permute-done.5 = f32[64,64]{1,0:T(8,128)S(1)} collective-permute-done((f32[64,64]{1,0:T(8,128)S(1)}, f32[64,64]{1,0:T(8,128)S(1)}, u32[]{:S(2)}, u32[]{:S(2)}) %collective-permute-start.5) | collective-permute-done | bytes 16416 | tf_op jit(solution)/shard_map/ppermute | solution.py:15
  190.0 5.8 %cholesky.185 = f32[64,64]{1,0:T(8,128)S(1)} custom-call(f32[64,64]{1,0:T(8,128)S(1)} %fusion.17), custom_call_target="Cholesky" | custom-call | tf_op jit(solution)/shard_map/jit(cholesky)/cholesky | solution.py:62
  195.9 0.6 compare_reduce_fusion
  196.5 0.7 fusion.12
  197.2 4.9 %custom-call.6 = f32[1,64,64]{1,2,0:T(8,128)S(1)} custom-call(f32[1,64,64]{2,1,0:T(8,128)S(1)} %fusion.12), custom_call_target="InvertDiagBlocksLowerTriangular" | custom-call | tf_op jit(solution)/shard_map/jit(_solve_triangular)/triangular_solve | solution.py:63
  202.1 0.9 fusion.3
  (43 shorter events, 2.3 us)
Async XLA Ops:
  6.5 3.8 %copy-start = (bf16[128,1024]{1,0:T(8,128)(2,1)S(1)}, bf16[128,1024]{1,0:T(8,128)(2,1)}, u32[]{:S(2)}) copy-start(bf16[128,1024]{1,0:T(8,128)(2,1)} %param.8) | copy-start | bytes 786436
  6.5 2.7 %copy-start.4 = (bf16[3584,128]{1,0:T(8,128)(2,1)S(1)}, bf16[3584,128]{1,0:T(8,128)(2,1)}, u32[]{:S(2)}) copy-start(bf16[3584,128]{1,0:T(8,128)(2,1)} %param.14) | copy-start | bytes 2752516
  6.5 2.7 %copy-start.5 = (bf16[128,3584]{1,0:T(8,128)(2,1)S(1)}, bf16[128,3584]{1,0:T(8,128)(2,1)}, u32[]{:S(2)}) copy-start(bf16[128,3584]{1,0:T(8,128)(2,1)} %param.9) | copy-start | bytes 2752516
  6.5 2.7 %copy-start.3 = (bf16[128,3584]{1,0:T(8,128)(2,1)S(1)}, bf16[128,3584]{1,0:T(8,128)(2,1)}, u32[]{:S(2)}) copy-start(bf16[128,3584]{1,0:T(8,128)(2,1)} %param.10) | copy-start | bytes 2752516
  6.5 85.0 %all-reduce.2.cloned.1.call-start = ((), (), s32[]{:S(2)}) async-start(), calls=%async_computation | async-start | bytes 262144 | tf_op jit(solution)/shard_map/psum | solution.py:51
  9.3 1.0 copy-start.1
  9.3 1.3 copy-start.2
  101.0 5.8 %collective-permute-start = (f32[64,64]{1,0:T(8,128)S(1)}, f32[64,64]{1,0:T(8,128)S(1)}, u32[]{:S(2)}, u32[]{:S(2)}) collective-permute-start(f32[64,64]{1,0:T(8,128)S(1)} %select_select_fusion.6), channel_id=1, source_target_pairs={{0,8},{8,0},{16,24},{24,16},{32,40},{40,32},{48,56},{56,48},{64,72... | collective-permute-start | bytes 49160 | tf_op jit(solution)/shard_map/ppermute | solution.py:15
  114.3 6.7 %collective-permute-start.1 = (f32[64,64]{1,0:T(8,128)S(1)}, f32[64,64]{1,0:T(8,128)S(1)}, u32[]{:S(2)}, u32[]{:S(2)}) collective-permute-start(f32[64,64]{1,0:T(8,128)S(1)} %select_select_fusion.5), channel_id=1, source_target_pairs={{0,16},{8,24},{16,0},{24,8},{32,48},{40,56},{48,32},{56,40},{64,80... | collective-permute-start | bytes 49160 | tf_op jit(solution)/shard_map/ppermute | solution.py:15
  128.4 9.7 %collective-permute-start.2 = (f32[64,64]{1,0:T(8,128)S(1)}, f32[64,64]{1,0:T(8,128)S(1)}, u32[]{:S(2)}, u32[]{:S(2)}) collective-permute-start(f32[64,64]{1,0:T(8,128)S(1)} %select_select_fusion.4), channel_id=1, source_target_pairs={{0,32},{8,40},{16,48},{24,56},{32,0},{40,8},{48,16},{56,24},{64,96... | collective-permute-start | bytes 49160 | tf_op jit(solution)/shard_map/ppermute | solution.py:15
  145.6 16.0 %collective-permute-start.3 = (f32[64,64]{1,0:T(8,128)S(1)}, f32[64,64]{1,0:T(8,128)S(1)}, u32[]{:S(2)}, u32[]{:S(2)}) collective-permute-start(f32[64,64]{1,0:T(8,128)S(1)} %select_select_fusion.3), channel_id=1, source_target_pairs={{0,64},{8,72},{16,80},{24,88},{32,96},{40,104},{48,112},{56,120},{... | collective-permute-start | bytes 49160 | tf_op jit(solution)/shard_map/ppermute | solution.py:15
  169.1 5.8 %collective-permute-start.4 = (f32[64,64]{1,0:T(8,128)S(1)}, f32[64,64]{1,0:T(8,128)S(1)}, u32[]{:S(2)}, u32[]{:S(2)}) collective-permute-start(f32[64,64]{1,0:T(8,128)S(1)} %select_select_fusion.2), channel_id=1, source_target_pairs={{0,128},{8,136},{16,144},{24,152},{32,160},{40,168},{48,176},{56,1... | collective-permute-start | bytes 49160 | tf_op jit(solution)/shard_map/ppermute | solution.py:15
  182.4 7.3 %collective-permute-start.5 = (f32[64,64]{1,0:T(8,128)S(1)}, f32[64,64]{1,0:T(8,128)S(1)}, u32[]{:S(2)}, u32[]{:S(2)}) collective-permute-start(f32[64,64]{1,0:T(8,128)S(1)} %select_select_fusion.1), channel_id=1, source_target_pairs={{0,256},{8,264},{16,272},{24,280},{32,288},{40,296},{48,304},{56,3... | collective-permute-start | bytes 49160 | tf_op jit(solution)/shard_map/ppermute | solution.py:15
Sparse Core Ops, SparseCore 0:
  11.8 79.6 all-reduce.1
where the time goes:
time: 210 us
  waiting for transfers between devices  93.9 us (45%)
  other arithmetic  55.8 us (27%)
  starting transfers between devices  36.1 us (17%)
  between operations  13.8 us (7%)
  matrix products  9.57 us (5%)
    psum x1, waiting for transfers between devices, shards(): summed = lax.psum(shaped, 'mp')  79.8 us
    another operation x18, other arithmetic, shards(): lower = jnp.linalg.cholesky(combined)  39.1 us
    ppermute x6, starting transfers between devices, partner_2(): return lax.ppermute(value, axis, pairs)  36.1 us
    ppermute x6, waiting for transfers between devices, partner_2(): return lax.ppermute(value, axis, pairs)  14.1 us
    another operation x3, other arithmetic, shards(): lower = jnp.linalg.cholesky(group_gram)  6.52 us
    another operation x2, other arithmetic, shards(): solved = jax.scipy.linalg.solve_triangular(lower, flat_mine.T, lower=True)  5.55 us
  transfers between devices with their start and end apart: 7, of which 7 were waited for; matrix products, arithmetic and copies ran while one was open for 1% of the time, Pallas kernels for 0%

commit v1 on v0

--- a/solution.py
+++ b/solution.py
@@ -48,7 +48,8 @@
     shaped = local_sums.reshape(local_examples, LEN, 4 * RANK)
     model_shards = lax.axis_size("mp")
     rows_each = 2 * RANK // model_shards
-    summed = lax.psum(shaped, "mp")
+    parts = lax.all_gather(shaped, "mp")
+    summed = jnp.sum(parts, axis=0)
     blocks = gradient_blocks(summed)
     mine = lax.dynamic_slice_in_dim(blocks, lax.axis_index("mp") * rows_each, rows_each, 1)
     group_gram = gram_of(blocks)

time: 210 us -> 166 us (0.79)
  waiting for transfers between devices: 93.9 us -> 49.5 us
    psum x1 -> x0, waiting for transfers between devices: 79.8 us -> none  [shards(): summed = lax.psum(shaped, 'mp')]
    all_gather x0 -> x1, waiting for transfers between devices: none -> 35.5 us  [shards(): parts = lax.all_gather(shaped, 'mp')]
where the time goes in v1:
time: 166 us
  other arithmetic  56.1 us (34%)
  waiting for transfers between devices  49.5 us (30%)
  starting transfers between devices  36.1 us (22%)
  between operations  13.8 us (8%)
  matrix products  8.03 us (5%)
  local copies, waits for them, and re-layouts  1.97 us (1%)
    another operation x18, other arithmetic, shards(): lower = jnp.linalg.cholesky(combined)  39.1 us
    ppermute x6, starting transfers between devices, partner_2(): return lax.ppermute(value, axis, pairs)  36.1 us
    all_gather x1, waiting for transfers between devices, shards(): parts = lax.all_gather(shaped, 'mp')  35.5 us
    ppermute x6, waiting for transfers between devices, partner_2(): return lax.ppermute(value, axis, pairs)  14 us
    another operation x3, other arithmetic, shards(): lower = jnp.linalg.cholesky(group_gram)  6.52 us
    another operation x2, other arithmetic, shards(): solved = jax.scipy.linalg.solve_triangular(lower, flat_mine.T, lower=True)  5.55 us
  transfers between devices with their start and end apart: 7, of which 7 were waited for; matrix products, arithmetic and copies ran while one was open for 1% of the time, Pallas kernels for 0%

profile of v1, /device:TPU:8, one launch (start us, length us, event | category | flops | bytes accessed | tf_op | source)
XLA Modules:
  0.0 165.5 jit_solution(14622303164799292180)
XLA Ops:
  6.6 2.7 %fusion.4 = f32[128,64]{0,1:T(8,128)S(1)} fusion(bf16[128,3584]{1,0:T(8,128)(2,1)} %param.11, bf16[3584,128]{1,0:T(8,128)(2,1)} %param.14, bf16[128,3584]{1,0:T(8,128)(2,1)} %param.9), kind=kOutput, calls=%fused_computation.18 | convolution fusion | flops 62390272 | bytes 2785280 | tf_op jit(solution)/shard_map/dot_general | solution.py:42
  9.3 1.0 fusion.5
  10.3 0.2 fusion.10
  10.6 0.4 fusion.8
  11.0 0.7 pad_maximum_fusion
  11.7 35.5 %all-gather.3.cloned.1.call-done = f32[1024,256]{0,1:T(8,128)} async-done(((f32[128,256]{0,1:T(8,128)}), f32[1024,256]{0,1:T(8,128)}) %all-gather.3.cloned.1.call-update) | async-done | bytes 1048592 | tf_op jit(solution)/shard_map/all_gather | solution.py:51
  47.1 1.4 copy.58
  48.5 0.3 bitcast_reduce_fusion
  49.2 0.3 fusion.15
  49.5 5.8 %cholesky.119 = f32[64,64]{1,0:T(8,128)S(1)} custom-call(f32[64,64]{1,0:T(8,128)S(1)} %fusion.23), custom_call_target="Cholesky" | custom-call | tf_op jit(solution)/shard_map/jit(cholesky)/cholesky | solution.py:57
  55.4 0.6 compare_reduce_fusion.6
  56.1 0.7 select_select_fusion.6
  56.7 3.5 %collective-permute-start = (f32[64,64]{1,0:T(8,128)S(1)}, f32[64,64]{1,0:T(8,128)S(1)}, u32[]{:S(2)}, u32[]{:S(2)}) collective-permute-start(f32[64,64]{1,0:T(8,128)S(1)} %select_select_fusion.6), channel_id=1, source_target_pairs={{0,8},{8,0},{16,24},{24,16},{32,40},{40,32},{48,56},{56,48},{64,72... | collective-permute-start | bytes 49160 | tf_op jit(solution)/shard_map/ppermute | solution.py:15
  60.4 2.1 %collective-permute-done = f32[64,64]{1,0:T(8,128)S(1)} collective-permute-done((f32[64,64]{1,0:T(8,128)S(1)}, f32[64,64]{1,0:T(8,128)S(1)}, u32[]{:S(2)}, u32[]{:S(2)}) %collective-permute-start) | collective-permute-done | bytes 16416 | tf_op jit(solution)/shard_map/ppermute | solution.py:15
  62.5 0.2 convolution_add_fusion.5
  62.8 5.8 %cholesky.130 = f32[64,64]{1,0:T(8,128)S(1)} custom-call(f32[64,64]{1,0:T(8,128)S(1)} %fusion.22), custom_call_target="Cholesky" | custom-call | tf_op jit(solution)/shard_map/jit(cholesky)/cholesky | solution.py:63
  68.7 0.6 compare_reduce_fusion.5
  69.4 0.7 select_select_fusion.5
  70.0 4.5 %collective-permute-start.1 = (f32[64,64]{1,0:T(8,128)S(1)}, f32[64,64]{1,0:T(8,128)S(1)}, u32[]{:S(2)}, u32[]{:S(2)}) collective-permute-start(f32[64,64]{1,0:T(8,128)S(1)} %select_select_fusion.5), channel_id=1, source_target_pairs={{0,16},{8,24},{16,0},{24,8},{32,48},{40,56},{48,32},{56,40},{64,80... | collective-permute-start | bytes 49160 | tf_op jit(solution)/shard_map/ppermute | solution.py:15
  74.7 2.1 %collective-permute-done.1 = f32[64,64]{1,0:T(8,128)S(1)} collective-permute-done((f32[64,64]{1,0:T(8,128)S(1)}, f32[64,64]{1,0:T(8,128)S(1)}, u32[]{:S(2)}, u32[]{:S(2)}) %collective-permute-start.1) | collective-permute-done | bytes 16416 | tf_op jit(solution)/shard_map/ppermute | solution.py:15
  76.7 0.2 convolution_add_fusion.4
  77.0 5.8 %cholesky.141 = f32[64,64]{1,0:T(8,128)S(1)} custom-call(f32[64,64]{1,0:T(8,128)S(1)} %fusion.21), custom_call_target="Cholesky" | custom-call | tf_op jit(solution)/shard_map/jit(cholesky)/cholesky | solution.py:63
  82.9 0.6 compare_reduce_fusion.4
  83.5 0.7 select_select_fusion.4
  84.2 7.6 %collective-permute-start.2 = (f32[64,64]{1,0:T(8,128)S(1)}, f32[64,64]{1,0:T(8,128)S(1)}, u32[]{:S(2)}, u32[]{:S(2)}) collective-permute-start(f32[64,64]{1,0:T(8,128)S(1)} %select_select_fusion.4), channel_id=1, source_target_pairs={{0,32},{8,40},{16,48},{24,56},{32,0},{40,8},{48,16},{56,24},{64,96... | collective-permute-start | bytes 49160 | tf_op jit(solution)/shard_map/ppermute | solution.py:15
  92.0 1.9 %collective-permute-done.2 = f32[64,64]{1,0:T(8,128)S(1)} collective-permute-done((f32[64,64]{1,0:T(8,128)S(1)}, f32[64,64]{1,0:T(8,128)S(1)}, u32[]{:S(2)}, u32[]{:S(2)}) %collective-permute-start.2) | collective-permute-done | bytes 16416 | tf_op jit(solution)/shard_map/ppermute | solution.py:15
  93.9 0.2 convolution_add_fusion.3
  94.2 5.8 %cholesky.152 = f32[64,64]{1,0:T(8,128)S(1)} custom-call(f32[64,64]{1,0:T(8,128)S(1)} %fusion.20), custom_call_target="Cholesky" | custom-call | tf_op jit(solution)/shard_map/jit(cholesky)/cholesky | solution.py:63
  100.1 0.6 compare_reduce_fusion.3
  100.7 0.7 select_select_fusion.3
  101.4 14.0 %collective-permute-start.3 = (f32[64,64]{1,0:T(8,128)S(1)}, f32[64,64]{1,0:T(8,128)S(1)}, u32[]{:S(2)}, u32[]{:S(2)}) collective-permute-start(f32[64,64]{1,0:T(8,128)S(1)} %select_select_fusion.3), channel_id=1, source_target_pairs={{0,64},{8,72},{16,80},{24,88},{32,96},{40,104},{48,112},{56,120},{... | collective-permute-start | bytes 49160 | tf_op jit(solution)/shard_map/ppermute | solution.py:15
  115.6 1.7 %collective-permute-done.3 = f32[64,64]{1,0:T(8,128)S(1)} collective-permute-done((f32[64,64]{1,0:T(8,128)S(1)}, f32[64,64]{1,0:T(8,128)S(1)}, u32[]{:S(2)}, u32[]{:S(2)}) %collective-permute-start.3) | collective-permute-done | bytes 16416 | tf_op jit(solution)/shard_map/ppermute | solution.py:15
  117.3 0.2 convolution_add_fusion.2
  117.6 5.8 %cholesky.163 = f32[64,64]{1,0:T(8,128)S(1)} custom-call(f32[64,64]{1,0:T(8,128)S(1)} %fusion.19), custom_call_target="Cholesky" | custom-call | tf_op jit(solution)/shard_map/jit(cholesky)/cholesky | solution.py:63
  123.5 0.6 compare_reduce_fusion.2
  124.1 0.7 select_select_fusion.2
  124.8 2.4 %collective-permute-start.4 = (f32[64,64]{1,0:T(8,128)S(1)}, f32[64,64]{1,0:T(8,128)S(1)}, u32[]{:S(2)}, u32[]{:S(2)}) collective-permute-start(f32[64,64]{1,0:T(8,128)S(1)} %select_select_fusion.2), channel_id=1, source_target_pairs={{0,128},{8,136},{16,144},{24,152},{32,160},{40,168},{48,176},{56,1... | collective-permute-start | bytes 49160 | tf_op jit(solution)/shard_map/ppermute | solution.py:15
  127.4 3.2 %collective-permute-done.4 = f32[64,64]{1,0:T(8,128)S(1)} collective-permute-done((f32[64,64]{1,0:T(8,128)S(1)}, f32[64,64]{1,0:T(8,128)S(1)}, u32[]{:S(2)}, u32[]{:S(2)}) %collective-permute-start.4) | collective-permute-done | bytes 16416 | tf_op jit(solution)/shard_map/ppermute | solution.py:15
  130.9 5.8 %cholesky.174 = f32[64,64]{1,0:T(8,128)S(1)} custom-call(f32[64,64]{1,0:T(8,128)S(1)} %fusion.18), custom_call_target="Cholesky" | custom-call | tf_op jit(solution)/shard_map/jit(cholesky)/cholesky | solution.py:63
  136.8 0.6 compare_reduce_fusion.1
  137.4 0.7 select_select_fusion.1
  138.1 4.0 %collective-permute-start.5 = (f32[64,64]{1,0:T(8,128)S(1)}, f32[64,64]{1,0:T(8,128)S(1)}, u32[]{:S(2)}, u32[]{:S(2)}) collective-permute-start(f32[64,64]{1,0:T(8,128)S(1)} %select_select_fusion.1), channel_id=1, source_target_pairs={{0,256},{8,264},{16,272},{24,280},{32,288},{40,296},{48,304},{56,3... | collective-permute-start | bytes 49160 | tf_op jit(solution)/shard_map/ppermute | solution.py:15
  142.3 3.1 %collective-permute-done.5 = f32[64,64]{1,0:T(8,128)S(1)} collective-permute-done((f32[64,64]{1,0:T(8,128)S(1)}, f32[64,64]{1,0:T(8,128)S(1)}, u32[]{:S(2)}, u32[]{:S(2)}) %collective-permute-start.5) | collective-permute-done | bytes 16416 | tf_op jit(solution)/shard_map/ppermute | solution.py:15
  145.7 5.8 %cholesky.185 = f32[64,64]{1,0:T(8,128)S(1)} custom-call(f32[64,64]{1,0:T(8,128)S(1)} %fusion.17), custom_call_target="Cholesky" | custom-call | tf_op jit(solution)/shard_map/jit(cholesky)/cholesky | solution.py:63
  151.6 0.6 compare_reduce_fusion
  152.2 0.7 fusion.12
  152.9 4.9 %custom-call.6 = f32[1,64,64]{1,2,0:T(8,128)S(1)} custom-call(f32[1,64,64]{2,1,0:T(8,128)S(1)} %fusion.12), custom_call_target="InvertDiagBlocksLowerTriangular" | custom-call | tf_op jit(solution)/shard_map/jit(_solve_triangular)/triangular_solve | solution.py:64
  157.8 0.9 fusion.3
  (45 shorter events, 2.7 us)
Async XLA Ops:
  6.5 3.8 %copy-start = (bf16[128,1024]{1,0:T(8,128)(2,1)S(1)}, bf16[128,1024]{1,0:T(8,128)(2,1)}, u32[]{:S(2)}) copy-start(bf16[128,1024]{1,0:T(8,128)(2,1)} %param.8) | copy-start | bytes 786436
  6.5 2.7 %copy-start.4 = (bf16[3584,128]{1,0:T(8,128)(2,1)S(1)}, bf16[3584,128]{1,0:T(8,128)(2,1)}, u32[]{:S(2)}) copy-start(bf16[3584,128]{1,0:T(8,128)(2,1)} %param.14) | copy-start | bytes 2752516
  6.5 2.7 %copy-start.5 = (bf16[128,3584]{1,0:T(8,128)(2,1)S(1)}, bf16[128,3584]{1,0:T(8,128)(2,1)}, u32[]{:S(2)}) copy-start(bf16[128,3584]{1,0:T(8,128)(2,1)} %param.9) | copy-start | bytes 2752516
  6.5 2.7 %copy-start.3 = (bf16[128,3584]{1,0:T(8,128)(2,1)S(1)}, bf16[128,3584]{1,0:T(8,128)(2,1)}, u32[]{:S(2)}) copy-start(bf16[128,3584]{1,0:T(8,128)(2,1)} %param.10) | copy-start | bytes 2752516
  6.5 40.6 %all-gather.3.cloned.1.call-start = ((), (), s32[]{:S(2)}) async-start(), calls=%async_computation | async-start | bytes 1179648 | tf_op jit(solution)/shard_map/all_gather | solution.py:51
  9.3 1.0 copy-start.1
  9.3 1.3 copy-start.2
  56.7 5.8 %collective-permute-start = (f32[64,64]{1,0:T(8,128)S(1)}, f32[64,64]{1,0:T(8,128)S(1)}, u32[]{:S(2)}, u32[]{:S(2)}) collective-permute-start(f32[64,64]{1,0:T(8,128)S(1)} %select_select_fusion.6), channel_id=1, source_target_pairs={{0,8},{8,0},{16,24},{24,16},{32,40},{40,32},{48,56},{56,48},{64,72... | collective-permute-start | bytes 49160 | tf_op jit(solution)/shard_map/ppermute | solution.py:15
  70.0 6.7 %collective-permute-start.1 = (f32[64,64]{1,0:T(8,128)S(1)}, f32[64,64]{1,0:T(8,128)S(1)}, u32[]{:S(2)}, u32[]{:S(2)}) collective-permute-start(f32[64,64]{1,0:T(8,128)S(1)} %select_select_fusion.5), channel_id=1, source_target_pairs={{0,16},{8,24},{16,0},{24,8},{32,48},{40,56},{48,32},{56,40},{64,80... | collective-permute-start | bytes 49160 | tf_op jit(solution)/shard_map/ppermute | solution.py:15
  84.2 9.7 %collective-permute-start.2 = (f32[64,64]{1,0:T(8,128)S(1)}, f32[64,64]{1,0:T(8,128)S(1)}, u32[]{:S(2)}, u32[]{:S(2)}) collective-permute-start(f32[64,64]{1,0:T(8,128)S(1)} %select_select_fusion.4), channel_id=1, source_target_pairs={{0,32},{8,40},{16,48},{24,56},{32,0},{40,8},{48,16},{56,24},{64,96... | collective-permute-start | bytes 49160 | tf_op jit(solution)/shard_map/ppermute | solution.py:15
  101.4 15.9 %collective-permute-start.3 = (f32[64,64]{1,0:T(8,128)S(1)}, f32[64,64]{1,0:T(8,128)S(1)}, u32[]{:S(2)}, u32[]{:S(2)}) collective-permute-start(f32[64,64]{1,0:T(8,128)S(1)} %select_select_fusion.3), channel_id=1, source_target_pairs={{0,64},{8,72},{16,80},{24,88},{32,96},{40,104},{48,112},{56,120},{... | collective-permute-start | bytes 49160 | tf_op jit(solution)/shard_map/ppermute | solution.py:15
  124.8 5.8 %collective-permute-start.4 = (f32[64,64]{1,0:T(8,128)S(1)}, f32[64,64]{1,0:T(8,128)S(1)}, u32[]{:S(2)}, u32[]{:S(2)}) collective-permute-start(f32[64,64]{1,0:T(8,128)S(1)} %select_select_fusion.2), channel_id=1, source_target_pairs={{0,128},{8,136},{16,144},{24,152},{32,160},{40,168},{48,176},{56,1... | collective-permute-start | bytes 49160 | tf_op jit(solution)/shard_map/ppermute | solution.py:15
  138.1 7.3 %collective-permute-start.5 = (f32[64,64]{1,0:T(8,128)S(1)}, f32[64,64]{1,0:T(8,128)S(1)}, u32[]{:S(2)}, u32[]{:S(2)}) collective-permute-start(f32[64,64]{1,0:T(8,128)S(1)} %select_select_fusion.1), channel_id=1, source_target_pairs={{0,256},{8,264},{16,272},{24,280},{32,288},{40,296},{48,304},{56,3... | collective-permute-start | bytes 49160 | tf_op jit(solution)/shard_map/ppermute | solution.py:15
Sparse Core Ops, SparseCore 0:
  11.8 35.2 all-gather.2
